TPU v7x, 32 devices: a whole 2x2x4 slice. The times are simulated.
32 devices in a mesh: space: 4 (over y, core), vel: 8 (over z, x).
Axes of the slice: x: 2, y: 2, z: 4, core: 2. Of those that a mesh axis runs over, the one named last changes fastest.
Arguments:
- distribution: float32 [4, 256, 13824], P('space', None, 'vel'), may hold values from -6 to 6
- neighbours: int32 [4, 4], P('space'), may hold values from -1 to 3, as said below
- block_level: int32 [4], P('space'), may hold values from 0 to 2
- collide_mask: int32 [1024], P('space'), may hold values from 0 to 1, as said below
- gain_first: float32 [6, 13824], replicated, may hold values from -1.8 to 1.8
- gain_second: float32 [6, 13824], replicated, may hold values from -1.8 to 1.8
- loss_rates: float32 [13824], replicated, may hold values from 0.2 to 2
Outputs:
- distribution_next: float32 [4, 256, 13824], P('space', None, 'vel')
Inputs may be any that keep to these rules, and one draw needn't show every extreme that they name: `neighbours`: each entry is -1 or a block held by the same index of space as the block itself or by the index one below or one above (index s holds blocks s * 1 to (s + 1) - 1). `collide_mask`: the cells of one index of space (its 1 block) hold at most 128 ones, and some index holds exactly 128.
All inputs are finite; a program needn't handle non-finite values.
Results may differ from a plain program's by a relative error of at most 0.0003.
Values sent between devices are 32-bit elements; how exact they have to be, the bound alone decides.
A program may use at most 128 MiB of HBM per device.

v0:
```python
import jax
import jax.numpy as jnp
from jax import lax
from jax.sharding import PartitionSpec as P

BSIDE = 16
VDIM = 24
ACT = 128
weno_eps = 1e-06
courant = 0.2


def extended(cells, sides, width):
    for axis, dim in sides:
        count = lax.axis_size(axis)
        ends = count - 1
        head = lax.slice_in_dim(cells, 0, width, axis=dim)
        tail = lax.slice_in_dim(cells, cells.shape[dim] - width, cells.shape[dim], axis=dim)
        cells = jnp.concatenate(
            [
                lax.ppermute(tail, axis, [(i, (i + 1) % count) for i in range(ends)]),
                cells,
                lax.ppermute(head, axis, [((i + 1) % count, i) for i in range(ends)]),
            ],
            axis=dim,
        )
    return cells


def weno_value(minus_two, minus_one, middle, plus_one, plus_two):
    guess_low = (2.0 * minus_two - 7.0 * minus_one + 11.0 * middle) / 6.0
    guess_mid = (-minus_one + 5.0 * middle + 2.0 * plus_one) / 6.0
    guess_high = (2.0 * middle + 5.0 * plus_one - plus_two) / 6.0
    rough_low = (
        13.0 / 12.0 * (minus_two - 2.0 * minus_one + middle) ** 2
        + 0.25 * (minus_two - 4.0 * minus_one + 3.0 * middle) ** 2
    )
    rough_mid = (
        13.0 / 12.0 * (minus_one - 2.0 * middle + plus_one) ** 2
        + 0.25 * (minus_one - plus_one) ** 2
    )
    rough_high = (
        13.0 / 12.0 * (middle - 2.0 * plus_one + plus_two) ** 2
        + 0.25 * (3.0 * middle - 4.0 * plus_one + plus_two) ** 2
    )
    weight_low = 0.1 / (weno_eps + rough_low) ** 2
    weight_mid = 0.6 / (weno_eps + rough_mid) ** 2
    weight_high = 0.3 / (weno_eps + rough_high) ** 2
    return (weight_low * guess_low + weight_mid * guess_mid + weight_high * guess_high) / (
        weight_low + weight_mid + weight_high
    )


def edge_values(padded, along, cell_count):

    def shifted(offset):
        return lax.slice_in_dim(padded, offset, offset + cell_count + 1, axis=along)

    upwind_low = weno_value(shifted(0), shifted(1), shifted(2), shifted(3), shifted(4))
    upwind_high = weno_value(shifted(5), shifted(4), shifted(3), shifted(2), shifted(1))
    return (upwind_low, upwind_high)


def flux_change(padded, along, cell_count, velocity):
    from_low, from_high = edge_values(padded, along, cell_count)
    step_low = lax.slice_in_dim(from_low, 1, cell_count + 1, axis=along) - lax.slice_in_dim(
        from_low, 0, cell_count, axis=along
    )
    step_high = lax.slice_in_dim(from_high, 1, cell_count + 1, axis=along) - lax.slice_in_dim(
        from_high, 0, cell_count, axis=along
    )
    return jnp.maximum(velocity, 0.0) * step_low + jnp.minimum(velocity, 0.0) * step_high


def transport_rate(
    padded_first, padded_second, along, cell_count, speed_first, speed_second, courant_ratio
):
    change = flux_change(padded_first, along, cell_count, speed_first) + flux_change(
        padded_second, along + 1, cell_count, speed_second
    )
    return -courant_ratio * change


def grid_speeds(vel_start, vel_width, vdim):
    index = vel_start + jnp.arange(vel_width, dtype=jnp.int32)
    first_index = index // (vdim * vdim)
    second_index = index // vdim % vdim
    half = (vdim - 1) / 2.0
    return (
        (first_index.astype(jnp.float32) - half) / half,
        (second_index.astype(jnp.float32) - half) / half,
    )


def hartley(length):
    grid_index = jnp.arange(length, dtype=jnp.float32)
    angle_table = 2.0 * jnp.pi * grid_index[:, None] * grid_index[None, :] / length
    return (jnp.cos(angle_table) + jnp.sin(angle_table)) / jnp.sqrt(jnp.float32(length))


def hartley_cube(velocity_cube, hartley_table):
    highest = lax.Precision.HIGHEST
    row_count, vdim = (velocity_cube.shape[0], hartley_table.shape[0])
    current = velocity_cube
    for turn in range(3):
        mapped = jnp.dot(
            current.reshape(-1, vdim),
            hartley_table,
            precision=highest,
            preferred_element_type=jnp.float32,
        )
        current = jnp.transpose(mapped.reshape(row_count, vdim, vdim, vdim), (0, 3, 1, 2))
    return current


def collide(cell_rows, gain_first, gain_second, loss_rates, hartley_table):
    row_count = cell_rows.shape[0]
    vdim = hartley_table.shape[0]
    terms = gain_first.shape[0]
    velocity_cube = cell_rows.reshape(row_count, vdim, vdim, vdim)
    spectrum = hartley_cube(velocity_cube, hartley_table)
    multipliers = jnp.concatenate([gain_first, gain_second, loss_rates[None]], axis=0).reshape(
        -1, 1, vdim, vdim, vdim
    )
    stacked = (spectrum[None] * multipliers).reshape(-1, vdim, vdim, vdim)
    images = hartley_cube(stacked, hartley_table).reshape(
        2 * terms + 1, row_count, vdim, vdim, vdim
    )
    gain_total = jnp.sum(images[:terms] * images[terms : 2 * terms], axis=0)
    loss_part = images[2 * terms]
    return (gain_total - velocity_cube * loss_part).reshape(row_count, -1)


def shards(
    distribution, neighbours, block_level, collide_mask, gain_first, gain_second, loss_rates
):
    blocks, cell_count, vel_width = distribution.shape
    block_side = BSIDE
    density = distribution.reshape(blocks, block_side, block_side, vel_width)
    vel_start = lax.axis_index("vel") * vel_width
    speed_first, speed_second = grid_speeds(vel_start, vel_width, VDIM)
    courant_ratio = (courant * jnp.exp2(block_level.astype(jnp.float32)))[:, None, None, None]
    pool_start = (lax.axis_index("space") - 1) * blocks
    present = (neighbours >= 0).astype(jnp.float32)
    pool_index = jnp.where(neighbours >= 0, neighbours - pool_start, blocks)

    def local_rate(current):
        strip_size = 3 * block_side * vel_width
        packed = jnp.concatenate(
            [
                current[:, :3].reshape(blocks, -1),
                current[:, block_side - 3 :].reshape(blocks, -1),
                current[:, :, :3].reshape(blocks, -1),
                current[:, :, block_side - 3 :].reshape(blocks, -1),
            ],
            axis=1,
        )
        ghost_pool = extended(packed, (("space", 0),), blocks)

        def select_face(face_index, strip_index):
            strips = ghost_pool[:, strip_index * strip_size : (strip_index + 1) * strip_size]
            return strips[pool_index[:, face_index]] * present[:, face_index][:, None]

        ghost_west = select_face(0, 1).reshape(blocks, 3, block_side, vel_width)
        ghost_east = select_face(1, 0).reshape(blocks, 3, block_side, vel_width)
        ghost_south = select_face(2, 3).reshape(blocks, block_side, 3, vel_width)
        ghost_north = select_face(3, 2).reshape(blocks, block_side, 3, vel_width)
        padded_first = jnp.concatenate([ghost_west, current, ghost_east], axis=1)
        padded_second = jnp.concatenate([ghost_south, current, ghost_north], axis=2)
        return transport_rate(
            padded_first, padded_second, 1, block_side, speed_first, speed_second, courant_ratio
        )

    section_one = density + local_rate(density)
    section_two = 0.5 * density + 0.5 * (section_one + local_rate(section_one))
    hartley_table = hartley(VDIM)
    flat_cells = section_two.reshape(blocks * cell_count, vel_width)
    vel_parts = lax.axis_size("vel")
    capacity = ACT
    chosen = jnp.nonzero(collide_mask, size=capacity, fill_value=0)[0]
    filled = (jnp.arange(capacity) < jnp.sum(collide_mask)).astype(jnp.float32)
    slot_rows = flat_cells[chosen] * filled[:, None]
    collided = collide(
        lax.all_to_all(
            slot_rows.reshape(vel_parts, -1, vel_width),
            "vel",
            split_axis=0,
            concat_axis=2,
            tiled=True,
        )[0],
        gain_first,
        gain_second,
        loss_rates,
        hartley_table,
    )
    change = lax.all_to_all(collided[None], "vel", split_axis=2, concat_axis=0, tiled=True)
    change = change.reshape(capacity, vel_width) * filled[:, None]
    result = flat_cells.at[chosen].add(change)
    return result.reshape(blocks, cell_count, vel_width)


def solution(mesh):
    in_specs = (P("space", None, "vel"), P("space", None), P("space"), P("space"), P(), P(), P())
    out_specs = P("space", None, "vel")
    return jax.shard_map(shards, mesh=mesh, in_specs=in_specs, out_specs=out_specs, check_vma=False)
```

profile of v0, /device:TPU:1, one launch (start us, length us, event | category | flops | bytes accessed | tf_op | source)
XLA Modules:
  0.0 621.4 jit_solution(15037906959466052470)
XLA Ops:
  11.1 4.8 collective-permute-start
  25.5 3.8 collective-permute-done.1
  30.4 4.8 pad_maximum_fusion
  35.2 2.4 fusion.207
  42.1 2.9 fusion.147
  46.1 2.9 fusion.148
  54.4 8.4 %fusion.111 = (f32[1,16,17,1728]{3,1,2,0:T(8,128)S(1)}, f32[1,16,17,1728]{3,1,2,0:T(8,128)S(1)}) fusion(f32[1,16,19,1728]{3,1,2,0:T(8,128)S(1)} %get-tuple-element.117, f32[1,16,19,1728]{3,1,2,0:T(8,128)S(1)} %copy_dynamic-update-slice_fusion.1), kind=kLoop, calls=%fused_computation.155 | loop fusion | flops 58281984 | bytes 15040512 | tf_op jit(solution)/shard_map/div | solution.py:49
  63.1 13.3 %fusion.60 = (f32[1,17,16,1728]{3,1,2,0:T(8,128)S(1)}, f32[1,17,16,1728]{3,1,2,0:T(8,128)S(1)}) fusion(f32[1,16,16,1728]{3,1,2,0:T(8,128)S(1)} %get-tuple-element.115, f32[1,3,16,1728]{3,1,2,0:T(4,128)S(1)} %copy-done.5, f32[1,19,16,1728]{3,1,2,0:T(8,128)S(1)} %copy_dynamic-update-slice_fusion), kind=kLoop, calls=%fused_computation.89 | loop fusion | flops 60162048 | bytes 11501568 | tf_op jit(solution)/shard_map/div | solution.py:49
  90.6 4.5 collective-permute-start.2
  100.5 8.2 %collective-permute-done.3 = f32[1,331776]{1,0:T(1,128)} collective-permute-done((f32[1,331776]{1,0:T(1,128)S(1)}, f32[1,331776]{1,0:T(1,128)}, u32[]{:S(2)}, u32[]{:S(2)}) %collective-permute-start.3) | collective-permute-done | bytes 1327136 | tf_op jit(solution)/shard_map/ppermute | solution.py:23
  109.8 5.4 pad_maximum_fusion.1
  117.2 4.0 fusion.145
  125.4 5.3 fusion.143
  132.4 15.2 %fusion.89 = (f32[1,16,17,1728]{3,1,2,0:T(8,128)S(1)}, f32[1,16,17,1728]{3,1,2,0:T(8,128)S(1)}) fusion(f32[1,16,16,1728]{3,1,2,0:T(8,128)} %copy-done, f32[1,16,3,1728]{3,1,2,0:T(8,128)S(1)} %copy.112, f32[1,16,3,1728]{3,1,2,0:T(8,128)S(1)} %copy.113), kind=kLoop, calls=%fused_computation.128 | loop fusion | flops 63452160 | bytes 6193152 | tf_op jit(solution)/shard_map/div | solution.py:49
  147.7 13.8 %fusion.34 = (f32[1,17,16,1728]{3,1,2,0:T(8,128)S(1)}, f32[1,17,16,1728]{3,1,2,0:T(8,128)S(1)}) fusion(f32[1,16,16,1728]{3,1,2,0:T(8,128)S(1)} %copy-done.1, f32[1,3,16,1728]{3,1,2,0:T(4,128)S(1)} %copy-done.7, f32[1,3,16,1728]{3,1,2,0:T(4,128)S(1)} %copy-done.6), kind=kLoop, calls=%fused_computation.58 | loop fusion | flops 63452160 | bytes 6193152 | tf_op jit(solution)/shard_map/div | solution.py:49
  161.6 2.7 fusion.129
  167.4 5.5 all-to-all-start
  173.2 2.5 concatenate.78
  175.7 3.5 concatenate.79
  179.1 4.3 maximum_bitcast_fusion
  183.4 3.5 all-to-all-done
  190.9 3.1 dot_general.20
  194.0 6.0 fusion.159
  200.1 9.5 %fusion.71 = f32[16,24,24,24]{1,2,3,0:T(8,128)} fusion(f32[16,24,24,24]{3,2,1,0:T(8,128)S(1)} %fusion.159, f32[24]{0:T(128)S(1)} %iota_multiply_fusion), kind=kOutput, calls=%fused_computation.102 | convolution fusion | flops 63703296 | bytes 1769568 | tf_op jit(solution)/shard_map/dot_general | solution.py:106
  209.5 6.3 %copy.121 = f32[16,24,24,24]{3,2,1,0:T(8,128)} copy(f32[16,24,24,24]{1,2,3,0:T(8,128)} %fusion.71) | data formatting | bytes 1769472 | tf_op jit(solution)/shard_map/transpose | solution.py:112
  215.8 7.6 %convolution_bitcast_fusion = f32[16,24,24,24]{1,3,2,0:T(8,128)} fusion(f32[16,24,24,24]{3,2,1,0:T(8,128)} %copy.121, f32[24]{0:T(128)S(1)} %iota_multiply_fusion), kind=kOutput, calls=%fused_computation.103 | convolution fusion | flops 63703296 | bytes 1769568 | tf_op jit(solution)/shard_map/dot_general | solution.py:106
  223.4 6.2 copy.123
  229.6 22.1 %broadcast_multiply_fusion = f32[13,16,24,24,24]{4,3,2,1,0:T(8,128)} fusion(f32[13,24,24,24]{3,2,1,0:T(8,128)} %maximum_bitcast_fusion, f32[16,24,24,24]{3,2,1,0:T(8,128)} %copy.123), kind=kLoop, calls=%fused_computation.5 | loop fusion | flops 2875392 | bytes 13105152 | tf_op jit(solution)/shard_map/mul | solution.py:125
  251.7 110.7 %fusion.12 = f32[208,24,24,24]{0,1,3,2:T(8,128)} fusion(f32[208,24,24,24]{3,2,1,0:T(8,128)} %bitcast.86, f32[24]{0:T(128)S(1)} %iota_multiply_fusion), kind=kOutput, calls=%fused_computation.12 | convolution fusion | flops 828115200 | bytes 23003232 | tf_op jit(solution)/shard_map/dot_general | solution.py:106
  362.4 21.1 %fusion.6 = f32[208,24,24,24]{0,1,3,2:T(8,128)S(1)} fusion(f32[208,24,24,24]{0,1,3,2:T(8,128)} %fusion.12, f32[24]{0:T(128)S(1)} %iota_multiply_fusion), kind=kOutput, calls=%fused_computation.10 | convolution fusion | flops 828115200 | bytes 23003232 | tf_op jit(solution)/shard_map/dot_general | solution.py:106
  383.6 19.6 %fusion.9 = f32[208,24,24,24]{0,1,3,2:T(8,128)} fusion(f32[208,24,24,24]{0,1,3,2:T(8,128)S(1)} %fusion.6, f32[24]{0:T(128)S(1)} %iota_multiply_fusion), kind=kOutput, calls=%fused_computation.11 | convolution fusion | flops 828115200 | bytes 23003232 | tf_op jit(solution)/shard_map/dot_general | solution.py:106
  403.2 11.8 %slice_multiply_fusion = f32[96,24,24,24]{0,1,3,2:T(8,128)} fusion(f32[208,24,24,24]{0,1,3,2:T(8,128)} %fusion.9), kind=kLoop, calls=%fused_computation.13 | loop fusion | flops 1327104 | bytes 15925248 | tf_op jit(solution)/shard_map/mul | solution.py:129
  415.0 7.7 %slice.449 = f32[16,24,24,24]{0,1,3,2:T(8,128)} slice(f32[208,24,24,24]{0,1,3,2:T(8,128)} %fusion.9), slice={[192:208], [0:24], [0:24], [0:24]} | slice | bytes 1769472 | tf_op jit(solution)/shard_map/slice | solution.py:130
  422.7 9.5 %copy.129 = f32[16,24,24,24]{3,2,1,0:T(8,128)} copy(f32[16,24,24,24]{0,1,3,2:T(8,128)} %slice.449) | data formatting | bytes 1769472 | tf_op jit(solution)/shard_map/slice | solution.py:130
  432.2 5.5 squeeze.23
  437.7 23.0 %copy.127 = f32[96,24,24,24]{3,2,1,0:T(8,128)} copy(f32[96,24,24,24]{0,1,3,2:T(8,128)} %slice_multiply_fusion) | data formatting | bytes 10616832 | tf_op jit(solution)/shard_map/mul | solution.py:129
  460.7 13.0 %reduce_sum.31 = f32[16,24,24,24]{3,2,1,0:T(8,128)} reduce(f32[6,16,24,24,24]{4,3,2,1,0:T(8,128)} %bitcast.90, f32[]{:T(128)} %constant.144.clone.1), dimensions={0}, to_apply=%region_6.7 | reduce | flops 1105920 | bytes 6193156 | tf_op jit(solution)/shard_map/reduce_sum | solution.py:129
  473.8 5.4 reduce_sum.32
  479.2 2.5 multiply_subtract_fusion.8
  481.6 13.4 %copy.130 = f32[1,16,13824]{1,0,2:T(1,128)} copy(f32[1,16,13824]{2,1,0:T(8,128)} %multiply_subtract_fusion.8) | data formatting | bytes 1769472 | tf_op jit(solution)/shard_map/sub | solution.py:131
  495.5 66.0 %reduce.36 = f32[13824,16]{1,0:T(8,128)} reduce(f32[13824,1,16]{2,1,0:T(1,128)} %bitcast.96, f32[]{:T(128)} %broadcast.820), dimensions={1}, to_apply=%bitcast.82.reduce_sub_computation | reduce | bytes 1769476
  561.5 5.8 reshape.653
  567.3 4.0 all-to-all-start.1
  571.9 16.0 %all-to-all-done.1 = f32[8,1,27648]{2,1,0:T(1,128)S(1)} async-done(((f32[8,1,27648]{2,1,0:T(1,128)}), f32[8,1,27648]{2,1,0:T(1,128)S(1)}, u32[]{:S(2)}, u32[]{:S(2)}) %all-to-all-start.1) | async-done | bytes 884768 | tf_op jit(solution)/shard_map/all_to_all | solution.py:196
  587.9 3.9 reduce.37
  591.8 19.7 %reshape.654 = f32[13824,1,16]{2,1,0:T(1,128)} reshape(f32[8,27648]{1,0:T(8,128)} %reduce.37) | data formatting | bytes 1769472
  611.5 4.8 copy.142
  616.9 2.7 scatter_fusion
  (131 shorter events, 63.9 us)
Async XLA Ops:
  4.2 11.7 %copy-start.22 = (s32[1,4]{1,0:T(1,128)S(1)}, s32[1,4]{1,0:T(1,128)}, u32[]{:S(2)}) copy-start(s32[1,4]{1,0:T(1,128)} %param.8) | copy-start | bytes 52
  9.2 20.1 %collective-permute-start.1 = (f32[1,331776]{1,0:T(1,128)S(1)}, f32[1,331776]{1,0:T(1,128)}, u32[]{:S(2)}, u32[]{:S(2)}) collective-permute-start(f32[1,331776]{1,0:T(1,128)S(1)} %constant_dynamic-update-slice_fusion), channel_id=1, source_target_pairs={{8,0},{16,8},{24,16},{9,1},{17,9},{25,17},{10,2},{18,10},{26,18},{... | collective-permute-start | bytes 3981320 | tf_op jit(solution)/shard_map/ppermute | solution.py:23
  11.1 19.2 %collective-permute-start = (f32[1,331776]{1,0:T(1,128)S(1)}, f32[1,331776]{1,0:T(1,128)}, u32[]{:S(2)}, u32[]{:S(2)}) collective-permute-start(f32[1,331776]{1,0:T(1,128)S(1)} %constant_dynamic-update-slice_fusion), channel_id=1, source_target_pairs={{0,8},{8,16},{16,24},{1,9},{9,17},{17,25},{2,10},{10,18},{18,26},{... | collective-permute-start | bytes 3981320 | tf_op jit(solution)/shard_map/ppermute | solution.py:21
  24.7 51.7 %copy-start.10 = (f32[1728]{0:T(1024)}, f32[1728]{0:T(1024)S(1)}, u32[]{:S(2)}) copy-start(f32[1728]{0:T(1024)S(1)} %broadcast_minimum_fusion.1) | copy-start | bytes 20740
  24.7 51.7 %copy-start.12 = (f32[1728]{0:T(1024)}, f32[1728]{0:T(1024)S(1)}, u32[]{:S(2)}) copy-start(f32[1728]{0:T(1024)S(1)} %broadcast_minimum_fusion) | copy-start | bytes 20740
  24.8 51.7 %copy-start.14 = (f32[1728]{0:T(1024)}, f32[1728]{0:T(1024)S(1)}, u32[]{:S(2)}) copy-start(f32[1728]{0:T(1024)S(1)} %broadcast_maximum_fusion) | copy-start | bytes 20740
  24.8 51.6 %copy-start.16 = (f32[1728]{0:T(1024)}, f32[1728]{0:T(1024)S(1)}, u32[]{:S(2)}) copy-start(f32[1728]{0:T(1024)S(1)} %broadcast_maximum_fusion.1) | copy-start | bytes 20740
  53.0 1.2 copy-start.4
  54.4 8.8 %copy-start.5 = (f32[1,3,16,1728]{3,1,2,0:T(4,128)S(1)}, f32[1,3,16,1728]{3,1,2,0:T(4,128)}, u32[]{:S(2)}) copy-start(f32[1,3,16,1728]{3,1,2,0:T(4,128)} %copy.97) | copy-start | bytes 995332
  78.8 1.3 copy-start
  83.3 5.4 copy-start.8
  84.4 10.7 %copy-start.21 = (s32[256]{0:T(256)S(1)}, s32[256]{0:T(256)}, u32[]{:S(2)}) copy-start(s32[256]{0:T(256)} %param.10) | copy-start | bytes 3076
  88.7 20.1 %collective-permute-start.3 = (f32[1,331776]{1,0:T(1,128)S(1)}, f32[1,331776]{1,0:T(1,128)}, u32[]{:S(2)}, u32[]{:S(2)}) collective-permute-start(f32[1,331776]{1,0:T(1,128)S(1)} %constant_dynamic-update-slice_fusion.7), channel_id=1, source_target_pairs={{8,0},{16,8},{24,16},{9,1},{17,9},{25,17},{10,2},{18,10},{26,18},{... | collective-permute-start | bytes 3981320 | tf_op jit(solution)/shard_map/ppermute | solution.py:23
  90.6 19.2 %collective-permute-start.2 = (f32[1,331776]{1,0:T(1,128)S(1)}, f32[1,331776]{1,0:T(1,128)}, u32[]{:S(2)}, u32[]{:S(2)}) collective-permute-start(f32[1,331776]{1,0:T(1,128)S(1)} %constant_dynamic-update-slice_fusion.7), channel_id=1, source_target_pairs={{0,8},{8,16},{16,24},{1,9},{9,17},{17,25},{2,10},{10,18},{18,26},{... | collective-permute-start | bytes 3981320 | tf_op jit(solution)/shard_map/ppermute | solution.py:21
  100.5 14.7 %copy-start.19 = (s32[128]{0:T(128)}, s32[128]{0:T(128)S(1)}, u32[]{:S(2)}) copy-start(s32[128]{0:T(128)S(1)} %fusion.153) | copy-start | bytes 1540
  132.4 15.2 %copy-start.1 = (f32[1,16,16,1728]{3,1,2,0:T(8,128)S(1)}, f32[1,16,16,1728]{3,1,2,0:T(8,128)}, u32[]{:S(2)}) copy-start(f32[1,16,16,1728]{3,1,2,0:T(8,128)} %copy-done) | copy-start | bytes 5308420
  132.4 15.2 %copy-start.6 = (f32[1,3,16,1728]{3,1,2,0:T(4,128)S(1)}, f32[1,3,16,1728]{3,1,2,0:T(4,128)}, u32[]{:S(2)}) copy-start(f32[1,3,16,1728]{3,1,2,0:T(4,128)} %copy.111) | copy-start | bytes 995332
  132.4 15.2 %copy-start.7 = (f32[1,3,16,1728]{3,1,2,0:T(4,128)S(1)}, f32[1,3,16,1728]{3,1,2,0:T(4,128)}, u32[]{:S(2)}) copy-start(f32[1,3,16,1728]{3,1,2,0:T(4,128)} %copy.110) | copy-start | bytes 995332
  147.7 13.9 %copy-start.11 = (f32[1728]{0:T(1024)S(1)}, f32[1728]{0:T(1024)}, u32[]{:S(2)}) copy-start(f32[1728]{0:T(1024)} %copy-done.10) | copy-start | bytes 20740
  147.7 13.9 %copy-start.13 = (f32[1728]{0:T(1024)S(1)}, f32[1728]{0:T(1024)}, u32[]{:S(2)}) copy-start(f32[1728]{0:T(1024)} %copy-done.12) | copy-start | bytes 20740
  147.7 13.9 %copy-start.15 = (f32[1728]{0:T(1024)S(1)}, f32[1728]{0:T(1024)}, u32[]{:S(2)}) copy-start(f32[1728]{0:T(1024)} %copy-done.14) | copy-start | bytes 20740
  147.7 13.9 %copy-start.17 = (f32[1728]{0:T(1024)S(1)}, f32[1728]{0:T(1024)}, u32[]{:S(2)}) copy-start(f32[1728]{0:T(1024)} %copy-done.16) | copy-start | bytes 20740
  166.3 6.6 %copy-start.18 = (f32[13824]{0:T(1024)S(1)}, f32[13824]{0:T(1024)}, u32[]{:S(2)}) copy-start(f32[13824]{0:T(1024)} %param.13) | copy-start | bytes 165892
  166.4 6.8 %copy-start.9 = (f32[6,13824]{1,0:T(8,128)S(1)}, f32[6,13824]{1,0:T(8,128)}, u32[]{:S(2)}) copy-start(f32[6,13824]{1,0:T(8,128)} %param.11) | copy-start | bytes 995332
  167.4 19.5 %all-to-all-start = ((f32[8,16,1728]{2,1,0:T(8,128)}), f32[8,16,1728]{2,1,0:T(8,128)S(1)}, u32[]{:S(2)}, u32[]{:S(2)}) async-start(f32[8,16,1728]{2,1,0:T(8,128)} %broadcast_multiply_fusion.1), calls=%async_computation | async-start | bytes 1835008 | tf_op jit(solution)/shard_map/all_to_all | solution.py:184
  186.9 0.9 copy-start.2
  473.8 5.4 copy-start.3
  567.3 20.7 %all-to-all-start.1 = ((f32[8,1,27648]{2,1,0:T(1,128)}), f32[8,1,27648]{2,1,0:T(1,128)S(1)}, u32[]{:S(2)}, u32[]{:S(2)}) async-start(f32[8,1,27648]{2,1,0:T(1,128)} %reshape.653), calls=%async_computation.1 | async-start | bytes 1769472 | tf_op jit(solution)/shard_map/all_to_all | solution.py:196
  616.3 0.6 copy-start.20
where the time goes:
time: 627 us; the launch traced here: 621 us
  other arithmetic  218 us (35%)
  matrix products  175 us (28%)
  local copies, waits for them, and re-layouts  163 us (26%)
  waiting for transfers between devices  33.7 us (5%)
  starting transfers between devices  22.6 us (4%)
  between operations  8.98 us (1%)
    dot_general x6, matrix products, hartley_cube(): jnp.dot(current.reshape(-1, vdim), hartley_table, precision=highest, pref...  175 us
    unnamed x1, other arithmetic  66 us
    div x4, other arithmetic, weno_value(): (weight_low * guess_low + weight_mid * guess_mid + weight_high * guess_hi...  50.8 us
    unnamed x57, local copies, waits for them, and re-layouts  37.3 us
    mul x2, other arithmetic, collide(): stacked = (spectrum[None] * multipliers).reshape(-1, vdim, vdim, vdim)  26.4 us
    mul x1, local copies, waits for them, and re-layouts, collide(): gain_total = jnp.sum(images[:terms] * images[terms:2 * terms], axis=0)  23 us
    mul x6, other arithmetic, select_face(): return strips[pool_index[:, face_index]] * present[:, face_index][:, None]  19.2 us
    slice x2, local copies, waits for them, and re-layouts, collide(): loss_part = images[2 * terms]  17.2 us
  transfers between devices with their start and end apart: 6, of which 6 were waited for; matrix products, arithmetic and copies ran while one was open for 3% of the time, Pallas kernels for 0%

commit v1 on v0

--- a/solution.py
+++ b/solution.py
@@ -193,7 +193,12 @@
         loss_rates,
         hartley_table,
     )
-    change = lax.all_to_all(collided[None], "vel", split_axis=2, concat_axis=0, tiled=True)
+    change = jnp.concatenate(
+        lax.all_to_all(
+            jnp.stack(jnp.split(collided[None], lax.axis_size("vel"), axis=2)), "vel", 0, 0
+        ),
+        axis=0,
+    )
     change = change.reshape(capacity, vel_width) * filled[:, None]
     result = flat_cells.at[chosen].add(change)
     return result.reshape(blocks, cell_count, vel_width)

time: 627 us -> 518 us (0.83)
  other arithmetic: 218 us -> 149 us
  local copies, waits for them, and re-layouts: 163 us -> 124 us
    unnamed x1 -> x0, other arithmetic: 66 us -> none
    unnamed x57, local copies, waits for them, and re-layouts: 37.3 us -> 16 us
    sub x1 -> x0, local copies, waits for them, and re-layouts: 13.4 us -> none  [collide(): return (gain_total - velocity_cube * loss_part).reshape(row_count, -1)]
where the time goes in v1:
time: 518 us; the launch traced here: 513 us
  matrix products  175 us (34%)
  other arithmetic  149 us (29%)
  local copies, waits for them, and re-layouts  124 us (24%)
  waiting for transfers between devices  34.2 us (7%)
  starting transfers between devices  22.5 us (4%)
  between operations  8.98 us (2%)
    dot_general x6, matrix products, hartley_cube(): jnp.dot(current.reshape(-1, vdim), hartley_table, precision=highest, pref...  175 us
    div x4, other arithmetic, weno_value(): (weight_low * guess_low + weight_mid * guess_mid + weight_high * guess_hi...  50.6 us
    mul x2, other arithmetic, collide(): stacked = (spectrum[None] * multipliers).reshape(-1, vdim, vdim, vdim)  26.4 us
    mul x1, local copies, waits for them, and re-layouts, collide(): gain_total = jnp.sum(images[:terms] * images[terms:2 * terms], axis=0)  23 us
    mul x6, other arithmetic, select_face(): return strips[pool_index[:, face_index]] * present[:, face_index][:, None]  19.2 us
    slice x2, local copies, waits for them, and re-layouts, collide(): loss_part = images[2 * terms]  17.2 us
    all_to_all x1, waiting for transfers between devices, shards(): lax.all_to_all(jnp.stack(jnp.split(collided[None], lax.axis_size('vel'),...  16.8 us
    unnamed x57, local copies, waits for them, and re-layouts  16 us
  transfers between devices with their start and end apart: 6, of which 6 were waited for; matrix products, arithmetic and copies ran while one was open for 3% of the time, Pallas kernels for 0%

profile of v1, /device:TPU:1, one launch (start us, length us, event | category | flops | bytes accessed | tf_op | source)
XLA Modules:
  0.0 513.3 jit_solution(9908777567664551467)
XLA Ops:
  0.0 1.8 copy.93
  9.2 1.9 collective-permute-start.1
  11.1 5.0 collective-permute-start
  25.8 3.5 collective-permute-done.1
  30.4 4.8 pad_maximum_fusion
  35.2 2.4 fusion.215
  37.6 2.4 fusion.150
  42.1 2.9 fusion.147
  46.1 2.9 fusion.148
  54.4 8.4 %fusion.111 = (f32[1,16,17,1728]{3,1,2,0:T(8,128)S(1)}, f32[1,16,17,1728]{3,1,2,0:T(8,128)S(1)}) fusion(f32[1,16,19,1728]{3,1,2,0:T(8,128)S(1)} %get-tuple-element.117, f32[1,16,19,1728]{3,1,2,0:T(8,128)S(1)} %copy_dynamic-update-slice_fusion.1), kind=kLoop, calls=%fused_computation.155 | loop fusion | flops 58281984 | bytes 15040512 | tf_op jit(solution)/shard_map/div | solution.py:49
  63.1 13.2 %fusion.60 = (f32[1,17,16,1728]{3,1,2,0:T(8,128)S(1)}, f32[1,17,16,1728]{3,1,2,0:T(8,128)S(1)}) fusion(f32[1,16,16,1728]{3,1,2,0:T(8,128)S(1)} %get-tuple-element.115, f32[1,3,16,1728]{3,1,2,0:T(4,128)S(1)} %copy-done.5, f32[1,19,16,1728]{3,1,2,0:T(8,128)S(1)} %copy_dynamic-update-slice_fusion), kind=kLoop, calls=%fused_computation.89 | loop fusion | flops 60162048 | bytes 11501568 | tf_op jit(solution)/shard_map/div | solution.py:49
  76.3 2.3 fusion.138
  88.6 1.9 collective-permute-start.3
  90.5 4.5 collective-permute-start.2
  95.7 2.3 scatter_custom_fusion
  100.3 8.3 %collective-permute-done.3 = f32[1,331776]{1,0:T(1,128)} collective-permute-done((f32[1,331776]{1,0:T(1,128)S(1)}, f32[1,331776]{1,0:T(1,128)}, u32[]{:S(2)}, u32[]{:S(2)}) %collective-permute-start.3) | collective-permute-done | bytes 1327136 | tf_op jit(solution)/shard_map/ppermute | solution.py:23
  109.7 5.0 pad_maximum_fusion.1
  114.8 2.0 fusion.214
  116.8 4.0 fusion.145
  124.9 5.3 %fusion.143 = (f32[82944]{0:T(1024)}, f32[82944]{0:T(1024)S(1)}) fusion(f32[3,82944]{1,0:T(4,128)S(1)} %get-tuple-element.96, s32[]{:T(128)} %bitcast.12, f32[]{:T(128)} %bitcast.13, f32[]{:T(128)} %bitcast.10, f32[3,82944]{1,0:T(4,128)} %get-tuple-element.97, s32[]{:T(128)} %bitcast.9), kind=kLoop, calls=%fused_computation.204 | loop fusion | flops 165888 | bytes 1327120 | tf_op jit(solution)/shard_map/mul | solution.py:162
  132.0 15.2 %fusion.89 = (f32[1,16,17,1728]{3,1,2,0:T(8,128)S(1)}, f32[1,16,17,1728]{3,1,2,0:T(8,128)S(1)}) fusion(f32[1,16,16,1728]{3,1,2,0:T(8,128)} %copy-done, f32[1,16,3,1728]{3,1,2,0:T(8,128)S(1)} %copy.109, f32[1,16,3,1728]{3,1,2,0:T(8,128)S(1)} %copy.110), kind=kLoop, calls=%fused_computation.128 | loop fusion | flops 63452160 | bytes 6193152 | tf_op jit(solution)/shard_map/div | solution.py:49
  147.3 13.8 %fusion.34 = (f32[1,17,16,1728]{3,1,2,0:T(8,128)S(1)}, f32[1,17,16,1728]{3,1,2,0:T(8,128)S(1)}) fusion(f32[1,16,16,1728]{3,1,2,0:T(8,128)S(1)} %copy-done.1, f32[1,3,16,1728]{3,1,2,0:T(4,128)S(1)} %copy-done.7, f32[1,3,16,1728]{3,1,2,0:T(4,128)S(1)} %copy-done.6), kind=kLoop, calls=%fused_computation.58 | loop fusion | flops 63452160 | bytes 6193152 | tf_op jit(solution)/shard_map/div | solution.py:49
  161.2 2.9 fusion.129
  167.3 5.5 %all-to-all-start = ((f32[8,16,1728]{2,1,0:T(8,128)}), f32[8,16,1728]{2,1,0:T(8,128)S(1)}, u32[]{:S(2)}, u32[]{:S(2)}) async-start(f32[8,16,1728]{2,1,0:T(8,128)} %broadcast_multiply_fusion.1), calls=%async_computation | async-start | bytes 1835008 | tf_op jit(solution)/shard_map/all_to_all | solution.py:184
  173.0 2.5 concatenate.78
  175.5 3.5 concatenate.79
  179.0 4.3 maximum_bitcast_fusion
  183.2 3.5 all-to-all-done
  190.7 3.1 dot_general.20
  193.8 6.1 %fusion.167 = f32[16,24,24,24]{3,2,1,0:T(8,128)S(1)} fusion(f32[16,24,24,24]{3,2,1,0:T(8,128)} %dot_general.20, f32[24]{0:T(128)S(1)} %iota_multiply_fusion), kind=kOutput, calls=%fused_computation.259 | convolution fusion | flops 63703296 | bytes 1769568 | tf_op jit(solution)/shard_map/dot_general | solution.py:106
  199.9 9.5 %fusion.71 = f32[16,24,24,24]{1,2,3,0:T(8,128)} fusion(f32[16,24,24,24]{3,2,1,0:T(8,128)S(1)} %fusion.167, f32[24]{0:T(128)S(1)} %iota_multiply_fusion), kind=kOutput, calls=%fused_computation.102 | convolution fusion | flops 63703296 | bytes 1769568 | tf_op jit(solution)/shard_map/dot_general | solution.py:106
  209.3 6.3 %copy.118 = f32[16,24,24,24]{3,2,1,0:T(8,128)} copy(f32[16,24,24,24]{1,2,3,0:T(8,128)} %fusion.71) | data formatting | bytes 1769472 | tf_op jit(solution)/shard_map/transpose | solution.py:112
  215.6 7.4 %convolution_bitcast_fusion = f32[16,24,24,24]{1,3,2,0:T(8,128)} fusion(f32[16,24,24,24]{3,2,1,0:T(8,128)} %copy.118, f32[24]{0:T(128)S(1)} %iota_multiply_fusion), kind=kOutput, calls=%fused_computation.103 | convolution fusion | flops 63703296 | bytes 1769568 | tf_op jit(solution)/shard_map/dot_general | solution.py:106
  223.0 6.2 %copy.120 = f32[16,24,24,24]{3,2,1,0:T(8,128)} copy(f32[16,24,24,24]{1,3,2,0:T(8,128)} %convolution_bitcast_fusion) | data formatting | bytes 1769472 | tf_op jit(solution)/shard_map/transpose | solution.py:112
  229.2 22.1 %broadcast_multiply_fusion = f32[13,16,24,24,24]{4,3,2,1,0:T(8,128)} fusion(f32[13,24,24,24]{3,2,1,0:T(8,128)} %maximum_bitcast_fusion, f32[16,24,24,24]{3,2,1,0:T(8,128)} %copy.120), kind=kLoop, calls=%fused_computation.5 | loop fusion | flops 2875392 | bytes 13105152 | tf_op jit(solution)/shard_map/mul | solution.py:125
  251.3 110.7 %fusion.12 = f32[208,24,24,24]{0,1,3,2:T(8,128)} fusion(f32[208,24,24,24]{3,2,1,0:T(8,128)} %bitcast.114, f32[24]{0:T(128)S(1)} %iota_multiply_fusion), kind=kOutput, calls=%fused_computation.12 | convolution fusion | flops 828115200 | bytes 23003232 | tf_op jit(solution)/shard_map/dot_general | solution.py:106
  362.0 21.1 %fusion.6 = f32[208,24,24,24]{0,1,3,2:T(8,128)S(1)} fusion(f32[208,24,24,24]{0,1,3,2:T(8,128)} %fusion.12, f32[24]{0:T(128)S(1)} %iota_multiply_fusion), kind=kOutput, calls=%fused_computation.10 | convolution fusion | flops 828115200 | bytes 23003232 | tf_op jit(solution)/shard_map/dot_general | solution.py:106
  383.2 19.9 %fusion.9 = f32[208,24,24,24]{0,1,3,2:T(8,128)} fusion(f32[208,24,24,24]{0,1,3,2:T(8,128)S(1)} %fusion.6, f32[24]{0:T(128)S(1)} %iota_multiply_fusion), kind=kOutput, calls=%fused_computation.11 | convolution fusion | flops 828115200 | bytes 23003232 | tf_op jit(solution)/shard_map/dot_general | solution.py:106
  403.0 11.8 %slice_multiply_fusion = f32[96,24,24,24]{0,1,3,2:T(8,128)} fusion(f32[208,24,24,24]{0,1,3,2:T(8,128)} %fusion.9), kind=kLoop, calls=%fused_computation.13 | loop fusion | flops 1327104 | bytes 15925248 | tf_op jit(solution)/shard_map/mul | solution.py:129
  414.8 7.7 %slice.449 = f32[16,24,24,24]{0,1,3,2:T(8,128)} slice(f32[208,24,24,24]{0,1,3,2:T(8,128)} %fusion.9), slice={[192:208], [0:24], [0:24], [0:24]} | slice | bytes 1769472 | tf_op jit(solution)/shard_map/slice | solution.py:130
  422.5 9.5 %copy.126 = f32[16,24,24,24]{3,2,1,0:T(8,128)} copy(f32[16,24,24,24]{0,1,3,2:T(8,128)} %slice.449) | data formatting | bytes 1769472 | tf_op jit(solution)/shard_map/slice | solution.py:130
  432.0 5.5 %squeeze.23 = f32[1,16,13824]{2,1,0:T(8,128)} reshape(f32[16,24,24,24]{3,2,1,0:T(8,128)} %copy.126) | data formatting | bytes 1769472 | tf_op jit(solution)/shard_map/squeeze | solution.py:130
  437.5 23.0 %copy.124 = f32[96,24,24,24]{3,2,1,0:T(8,128)} copy(f32[96,24,24,24]{0,1,3,2:T(8,128)} %slice_multiply_fusion) | data formatting | bytes 10616832 | tf_op jit(solution)/shard_map/mul | solution.py:129
  460.5 13.0 %reduce_sum.31 = f32[16,24,24,24]{3,2,1,0:T(8,128)} reduce(f32[6,16,24,24,24]{4,3,2,1,0:T(8,128)} %bitcast.118, f32[]{:T(128)} %constant.144.clone.1), dimensions={0}, to_apply=%region_6.7 | reduce | flops 1105920 | bytes 6193156 | tf_op jit(solution)/shard_map/reduce_sum | solution.py:129
  473.6 5.4 %reduce_sum.32 = f32[1,16,13824]{2,1,0:T(8,128)} reshape(f32[16,24,24,24]{3,2,1,0:T(8,128)} %reduce_sum.31) | data formatting | bytes 1769472 | tf_op jit(solution)/shard_map/reduce_sum | solution.py:129
  486.1 3.6 all-to-all-start.1
  490.3 16.8 %all-to-all-done.1 = f32[8,1,16,1728]{3,2,1,0:T(8,128)S(1)} async-done(((f32[8,1,16,1728]{3,2,1,0:T(8,128)}), f32[8,1,16,1728]{3,2,1,0:T(8,128)S(1)}, u32[]{:S(2)}, u32[]{:S(2)}) %all-to-all-start.1) | async-done | bytes 884768 | tf_op jit(solution)/shard_map/all_to_all | solution.py:197
  508.1 3.3 scatter_fusion
  (127 shorter events, 56.2 us)
Async XLA Ops:
  4.2 11.9 %copy-start.20 = (s32[1,4]{1,0:T(1,128)S(1)}, s32[1,4]{1,0:T(1,128)}, u32[]{:S(2)}) copy-start(s32[1,4]{1,0:T(1,128)} %param.8) | copy-start | bytes 52
  9.2 20.1 %collective-permute-start.1 = (f32[1,331776]{1,0:T(1,128)S(1)}, f32[1,331776]{1,0:T(1,128)}, u32[]{:S(2)}, u32[]{:S(2)}) collective-permute-start(f32[1,331776]{1,0:T(1,128)S(1)} %constant_dynamic-update-slice_fusion), channel_id=1, source_target_pairs={{8,0},{16,8},{24,16},{9,1},{17,9},{25,17},{10,2},{18,10},{26,18},{... | collective-permute-start | bytes 3981320 | tf_op jit(solution)/shard_map/ppermute | solution.py:23
  11.1 19.2 %collective-permute-start = (f32[1,331776]{1,0:T(1,128)S(1)}, f32[1,331776]{1,0:T(1,128)}, u32[]{:S(2)}, u32[]{:S(2)}) collective-permute-start(f32[1,331776]{1,0:T(1,128)S(1)} %constant_dynamic-update-slice_fusion), channel_id=1, source_target_pairs={{0,8},{8,16},{16,24},{1,9},{9,17},{17,25},{2,10},{10,18},{18,26},{... | collective-permute-start | bytes 3981320 | tf_op jit(solution)/shard_map/ppermute | solution.py:21
  25.0 51.3 %copy-start.10 = (f32[1728]{0:T(1024)}, f32[1728]{0:T(1024)S(1)}, u32[]{:S(2)}) copy-start(f32[1728]{0:T(1024)S(1)} %broadcast_minimum_fusion.1) | copy-start | bytes 20740
  25.0 51.3 %copy-start.12 = (f32[1728]{0:T(1024)}, f32[1728]{0:T(1024)S(1)}, u32[]{:S(2)}) copy-start(f32[1728]{0:T(1024)S(1)} %broadcast_minimum_fusion) | copy-start | bytes 20740
  25.1 51.3 %copy-start.14 = (f32[1728]{0:T(1024)}, f32[1728]{0:T(1024)S(1)}, u32[]{:S(2)}) copy-start(f32[1728]{0:T(1024)S(1)} %broadcast_maximum_fusion) | copy-start | bytes 20740
  25.1 51.3 %copy-start.16 = (f32[1728]{0:T(1024)}, f32[1728]{0:T(1024)S(1)}, u32[]{:S(2)}) copy-start(f32[1728]{0:T(1024)S(1)} %broadcast_maximum_fusion.1) | copy-start | bytes 20740
  53.0 1.2 copy-start.4
  54.4 8.8 %copy-start.5 = (f32[1,3,16,1728]{3,1,2,0:T(4,128)S(1)}, f32[1,3,16,1728]{3,1,2,0:T(4,128)}, u32[]{:S(2)}) copy-start(f32[1,3,16,1728]{3,1,2,0:T(4,128)} %copy.94) | copy-start | bytes 995332
  78.6 1.3 copy-start
  83.2 5.4 %copy-start.8 = (f32[1,82944]{1,0:T(1,128)S(1)}, f32[1,82944]{1,0:T(1,128)}, u32[]{:S(2)}) copy-start(f32[1,82944]{1,0:T(1,128)} %reshape.412) | copy-start | bytes 995332
  84.3 10.7 %copy-start.19 = (s32[256]{0:T(256)S(1)}, s32[256]{0:T(256)}, u32[]{:S(2)}) copy-start(s32[256]{0:T(256)} %param.10) | copy-start | bytes 3076
  88.6 20.1 %collective-permute-start.3 = (f32[1,331776]{1,0:T(1,128)S(1)}, f32[1,331776]{1,0:T(1,128)}, u32[]{:S(2)}, u32[]{:S(2)}) collective-permute-start(f32[1,331776]{1,0:T(1,128)S(1)} %constant_dynamic-update-slice_fusion.7), channel_id=1, source_target_pairs={{8,0},{16,8},{24,16},{9,1},{17,9},{25,17},{10,2},{18,10},{26,18},{... | collective-permute-start | bytes 3981320 | tf_op jit(solution)/shard_map/ppermute | solution.py:23
  90.5 19.2 %collective-permute-start.2 = (f32[1,331776]{1,0:T(1,128)S(1)}, f32[1,331776]{1,0:T(1,128)}, u32[]{:S(2)}, u32[]{:S(2)}) collective-permute-start(f32[1,331776]{1,0:T(1,128)S(1)} %constant_dynamic-update-slice_fusion.7), channel_id=1, source_target_pairs={{0,8},{8,16},{16,24},{1,9},{9,17},{17,25},{2,10},{10,18},{18,26},{... | collective-permute-start | bytes 3981320 | tf_op jit(solution)/shard_map/ppermute | solution.py:21
  132.0 15.2 %copy-start.1 = (f32[1,16,16,1728]{3,1,2,0:T(8,128)S(1)}, f32[1,16,16,1728]{3,1,2,0:T(8,128)}, u32[]{:S(2)}) copy-start(f32[1,16,16,1728]{3,1,2,0:T(8,128)} %copy-done) | copy-start | bytes 5308420
  132.0 15.2 %copy-start.6 = (f32[1,3,16,1728]{3,1,2,0:T(4,128)S(1)}, f32[1,3,16,1728]{3,1,2,0:T(4,128)}, u32[]{:S(2)}) copy-start(f32[1,3,16,1728]{3,1,2,0:T(4,128)} %copy.108) | copy-start | bytes 995332
  132.0 15.2 %copy-start.7 = (f32[1,3,16,1728]{3,1,2,0:T(4,128)S(1)}, f32[1,3,16,1728]{3,1,2,0:T(4,128)}, u32[]{:S(2)}) copy-start(f32[1,3,16,1728]{3,1,2,0:T(4,128)} %copy.107) | copy-start | bytes 995332
  147.3 13.9 %copy-start.11 = (f32[1728]{0:T(1024)S(1)}, f32[1728]{0:T(1024)}, u32[]{:S(2)}) copy-start(f32[1728]{0:T(1024)} %copy-done.10) | copy-start | bytes 20740
  147.3 13.9 %copy-start.13 = (f32[1728]{0:T(1024)S(1)}, f32[1728]{0:T(1024)}, u32[]{:S(2)}) copy-start(f32[1728]{0:T(1024)} %copy-done.12) | copy-start | bytes 20740
  147.3 13.9 %copy-start.15 = (f32[1728]{0:T(1024)S(1)}, f32[1728]{0:T(1024)}, u32[]{:S(2)}) copy-start(f32[1728]{0:T(1024)} %copy-done.14) | copy-start | bytes 20740
  147.3 13.9 %copy-start.17 = (f32[1728]{0:T(1024)S(1)}, f32[1728]{0:T(1024)}, u32[]{:S(2)}) copy-start(f32[1728]{0:T(1024)} %copy-done.16) | copy-start | bytes 20740
  166.2 6.6 %copy-start.18 = (f32[13824]{0:T(1024)S(1)}, f32[13824]{0:T(1024)}, u32[]{:S(2)}) copy-start(f32[13824]{0:T(1024)} %param.13) | copy-start | bytes 165892
  166.2 6.8 %copy-start.9 = (f32[6,13824]{1,0:T(8,128)S(1)}, f32[6,13824]{1,0:T(8,128)}, u32[]{:S(2)}) copy-start(f32[6,13824]{1,0:T(8,128)} %param.11) | copy-start | bytes 995332
  167.3 19.4 %all-to-all-start = ((f32[8,16,1728]{2,1,0:T(8,128)}), f32[8,16,1728]{2,1,0:T(8,128)S(1)}, u32[]{:S(2)}, u32[]{:S(2)}) async-start(f32[8,16,1728]{2,1,0:T(8,128)} %broadcast_multiply_fusion.1), calls=%async_computation | async-start | bytes 1835008 | tf_op jit(solution)/shard_map/all_to_all | solution.py:184
  186.7 0.9 copy-start.2
  473.6 5.4 %copy-start.3 = (f32[1,16,13824]{2,1,0:T(8,128)S(1)}, f32[1,16,13824]{2,1,0:T(8,128)}, u32[]{:S(2)}) copy-start(f32[1,16,13824]{2,1,0:T(8,128)} %reshape_squeeze.3) | copy-start | bytes 2654212
  486.1 21.0 %all-to-all-start.1 = ((f32[8,1,16,1728]{3,2,1,0:T(8,128)}), f32[8,1,16,1728]{3,2,1,0:T(8,128)S(1)}, u32[]{:S(2)}, u32[]{:S(2)}) async-start(f32[8,1,16,1728]{3,2,1,0:T(8,128)} %fusion.151), calls=%async_computation.1 | async-start | bytes 1835008 | tf_op jit(solution)/shard_map/all_to_all | solution.py:197
